TPU v7x, 256 devices: a whole 4x4x8 slice. The times are simulated.
256 devices in a mesh: comp: 2 (over x_lo), ox: 16 (over x_hi, y, core), oy: 8 (over z).
Axes of the slice: x: 4 (x_hi: 2, x_lo: 2; x = x_hi * 2 + x_lo), y: 4, z: 8, core: 2. Of those that a mesh axis runs over, the one named last changes fastest.
Arguments:
- atmos_stress: float32 [2, 2359296], P(None, ('comp', 'ox', 'oy')), may hold values from -6 to 6
- route_tile: int32 [2359296, 1], P(('comp', 'ox', 'oy')), may hold values from 0 to 255; in each aligned block of 9216 rows (0 to 9215, 9216 to 18431, ...) at most 144 rows name the same one
- route_cell: int32 [2359296], P(('comp', 'ox', 'oy')), may hold values from 0 to 54674
- route_weight: float32 [2359296], P(('comp', 'ox', 'oy')), may hold values from 0.25 to 1
- velocity: float32 [2, 8, 4320, 3240], P(None, None, ('comp', 'ox'), 'oy'), may hold values from -6 to 6
- thickness: float32 [8, 4320, 3240], P(None, ('comp', 'ox'), 'oy'), may hold values from 0.5 to 2
- coriolis: float32 [4320, 3240], P(('comp', 'ox'), 'oy'), may hold values from -0.5 to 0.5
- ocean_axes: float32 [2, 3, 4320, 3240], P(None, None, ('comp', 'ox'), 'oy'), may hold values from -3 to 3
- ocean_mask: int32 [4320, 3240], P(('comp', 'ox'), 'oy'), may hold values 0 or 1
Outputs:
- new_velocity: float32 [2, 8, 4320, 3240], P(None, None, ('comp', 'ox'), 'oy')
Inputs may be any that keep to these rules, and one draw needn't show every extreme that they name: `route_tile`: tiles are numbered as devices, comp-major, then ox, then oy. Of the 9216 cells of one device, at most 144 name the same tile, and on some device exactly 144 do.
All inputs are finite; a program needn't handle non-finite values. No bound on the sum of `ocean_mask` on one device may be relied on, other than what follows from the above.
Results may differ from a plain program's by a relative error of at most 0.0003.
Values sent between devices are 32-bit elements; how exact they have to be, the bound alone decides.
A program may use at most 128 MiB of HBM per device.

v0:
```python
import math

import jax
import jax.numpy as jnp
from jax import lax
from jax.experimental import pallas as pl
from jax.experimental.pallas import tpu as pltpu
from jax.sharding import PartitionSpec as P

BF = jnp.bfloat16
F32 = jnp.float32
I32 = jnp.int32
MESH = pl.DeviceIdType.MESH
FN=[[1,0,0],[0,1,0],[-1,0,0],[0,-1,0],[0,0,1],[0,0,-1]]
FA=[[0,1,0],[-1,0,0],[0,-1,0],[1,0,0],[0,1,0],[0,1,0]]
FB=[[0,0,1],[0,0,1],[0,0,1],[0,0,1],[-1,0,0],[1,0,0]]

def tan_small(t):
    u=t*t
    s=t*(1.0+u*(-1/6.0+u*(1/120.0+u*(-1/5040.0+u*(1/362880.0)))))
    c=1.0+u*(-0.5+u*(1/24.0+u*(-1/720.0+u*(1/40320.0+u*(-1/3628800.0)))))
    return s/c

def pack_kernel(pos_ref, stress_ref, tile_ref, cell_ref, weight_ref, out_ref, tout_ref, key_s, val_s, tr_s):
    comp=pos_ref[0]; ox=pos_ref[1]; oy=pos_ref[2]
    for f in range(3):
        rows=pl.ds(24*f,24)
        sub=lax.broadcasted_iota(I32,(24,128),0); lane=lax.broadcasted_iota(I32,(24,128),1)
        crow=ox*48+2*sub+lane//64
        ccol=oy*64+lane%64
        p=tan_small((crow.astype(F32)+0.5)*(0.5*math.pi/768)-0.25*math.pi)
        q=tan_small((ccol.astype(F32)+0.5)*(0.5*math.pi/512)-0.25*math.pi)
        pp=1.0+p*p; qq=1.0+q*q; rs=lax.rsqrt(pp+q*q)
        w=weight_ref[rows,:]*rs
        u=stress_ref[rows,0,:]*w*lax.rsqrt(qq)
        v=stress_ref[rows,1,:]*w*lax.rsqrt(pp)
        N=-(p*u+q*v); A=qq*u-p*q*v; B=pp*v-p*q*u
        for c in range(3):
            def coef(T): return jnp.where(comp==0,float(T[f][c]),float(T[f+3][c])).astype(F32)
            val_s[c,rows,:]=N*coef(FN)+A*coef(FA)+B*coef(FB)
    key_s[...]=tile_ref[...]*65536+cell_ref[...]
    tid=lax.broadcasted_iota(I32,(256,128),0)
    def cnt(r,acc):
        rows=tile_ref[pl.ds(pl.multiple_of(8*r,8),8),:]
        for k in range(8):
            acc=acc+jnp.where(jnp.broadcast_to(rows[k:k+1,:],(256,128))<tid,1.0,0.0)
        return acc
    acc=lax.fori_loop(0,9,cnt,jnp.zeros((256,128),F32))
    start=jnp.sum(acc,axis=1,keepdims=True)
    keys=[key_s[pl.ds(8*i,8),:] for i in range(9)]+[jnp.full((8,128),2**31-1,I32)]*7
    vals=[[val_s[c,pl.ds(8*i,8),:] for i in range(9)]+[jnp.zeros((8,128),F32)]*7 for c in range(3)]
    lane=lax.broadcasted_iota(I32,(8,128),1); sub=lax.broadcasted_iota(I32,(8,128),0)
    arrs=[keys]+vals
    def bitmask(b):
        if b<3: return (sub>>b)&1
        if b<7: return [bool((i>>(b-3))&1) for i in range(16)]
        return (lane>>(b-7))&1
    for kk in range(1,15):
        for j in reversed(range(kk)):
            dirbits=bitmask(kk) if kk<14 else [False]*16
            if 3<=j<7:
                new=[[None]*16 for _ in arrs]
                for i in range(16):
                    if (i>>(j-3))&1: continue
                    h=i|(1<<(j-3))
                    a,b=arrs[0][i],arrs[0][h]
                    gt=a>b
                    if isinstance(dirbits,list):
                        swap=(b>a) if dirbits[i] else gt
                    else:
                        swap=jnp.where(dirbits==1,b-a,a-b)>0
                    for n in range(4):
                        x,y=arrs[n][i],arrs[n][h]
                        new[n][i]=jnp.where(swap,y,x); new[n][h]=jnp.where(swap,x,y)
                arrs=new
            else:
                bit=bitmask(j)
                if isinstance(dirbits,list): sgn=None
                new=[[None]*16 for _ in arrs]
                if j<3:
                    d=1<<j
                    part=lambda x: jnp.where(bit==1,pltpu.roll(x,d,0),pltpu.roll(x,8-d,0)) if d<4 else pltpu.roll(x,4,0)
                else:
                    d=1<<(j-7)
                    if d==64: part=lambda x: pltpu.roll(x,64,1)
                    else: part=lambda x: jnp.take_along_axis(x,lane^d,axis=1,mode="promise_in_bounds")
                for i in range(16):
                    k=arrs[0][i]; pk=part(k)
                    if isinstance(dirbits,list): flip=bit^(1 if dirbits[i] else 0)
                    else: flip=bit^dirbits
                    take=jnp.where(flip==1,pk-k,k-pk)>0
                    new[0][i]=jnp.where(take,pk,k)
                    for n in range(1,4):
                        x=arrs[n][i]
                        new[n][i]=jnp.where(take,part(x),x)
                arrs=new
    turned=[None]*4
    for n in range(4):
        for v in range(16):
            x=arrs[n][v]
            if n==0: x=(x&65535).astype(F32)
            tr_s[pl.ds(8*v,8),:]=x
        turned[3 if n==0 else n-1]=tr_s[...].T
    table=jnp.concatenate(turned,axis=1)
    p0=table.astype(BF); d0=table-p0.astype(F32)
    p1=d0.astype(BF); p2=(d0-p1.astype(F32)).astype(BF)
    lane=lax.broadcasted_iota(I32,(256,128),1).astype(F32)
    start=jnp.broadcast_to(start,(256,128))
    row=jnp.floor(start*(1.0/128)); off=start-128.0*row
    last=lax.broadcasted_iota(I32,(256,128),0)==255
    left=jnp.where(last,9216.0,pltpu.roll(start,255,0))-start
    got=[]
    for k in range(3):
        pick=jnp.where(lane==row+float(k),1.0,0.0).astype(BF)
        got.append(sum(jnp.dot(pick,q,preferred_element_type=F32) for q in (p0,p1,p2)))
    at=(lane+off).astype(I32)&127
    inlo=lane+off<128.0
    tl=jnp.zeros((256,128),F32)
    for c in range(4):
        y0,y1,y2=[jnp.take_along_axis(g[:,128*c:128*c+128],at,axis=1,mode="promise_in_bounds") for g in got]
        fill=-1.0 if c==3 else 0.0
        out_ref[:,c,:]=jnp.where(lane<left,jnp.where(inlo,y0,y1),fill)
        g=jnp.where(lane+128.0<left,jnp.where(inlo,y1,y2),fill)
        if c: g=pltpu.roll(g,16*c,1)
        tl=jnp.where((lane>=16.0*c)&(lane<16.0*c+16.0),g,tl)
    tout_ref[:,0,:]=tl

W=80; SL=8; AR=304
def unpack_prepare(rec_ref, tail_ref, ent, mm_v):
    lane=lax.broadcasted_iota(I32,(256,128),1)
    tail=tail_ref[:,0,:]
    cellm=rec_ref[:,3,:]
    cellt=pltpu.roll(tail,80,1)
    n=jnp.sum(jnp.where(cellm>=0,1.0,0.0),axis=1,keepdims=True)+jnp.sum(jnp.where((cellt>=0)&(lane<16),1.0,0.0),axis=1,keepdims=True)
    S=jnp.maximum(jnp.max(n),1.0)
    def where_from(l):
        f=jnp.minimum(jnp.floor((l.astype(F32)*n+0.5)/S),143.0)
        g=jnp.minimum(jnp.floor(((l-1).astype(F32)*n+0.5)/S),143.0)
        return f,((f!=g)|(l==0))&(l.astype(F32)<S)&(n>0)
    fm,okm=where_from(lane)
    ft,okt=where_from(lane%16+128)
    fmi=jnp.clip(fm.astype(I32),0,127); fti=jnp.clip(ft.astype(I32),0,143)
    lo_i=jnp.minimum(fti,127)
    intail=fti>=128
    for c in (3,0,1,2):
        main=rec_ref[:,c,:]
        t=pltpu.roll(tail,(128-16*c)%128,1) if c else tail
        m2=jnp.take_along_axis(main,fmi,axis=1,mode="promise_in_bounds")
        ta=jnp.take_along_axis(main,lo_i,axis=1,mode="promise_in_bounds")
        tb=jnp.take_along_axis(t,jnp.where(intail,fti-128,0),axis=1,mode="promise_in_bounds")
        t2=jnp.where(intail,tb,ta)
        if c==3:
            m2=jnp.where(okm,m2,-1.0); t2=jnp.where(okt,t2,-1.0)
            for q,x in enumerate((m2,t2)):
                a=jnp.floor((x+0.5)*(1/256.0))
                mn=jnp.min(jnp.where(x>=0,a,999.0),axis=0,keepdims=True)
                mx=jnp.max(a,axis=0,keepdims=True)
                mm_v[pl.ds(0,1),pl.ds(128*q,128)]=mn.astype(I32)
                mm_v[pl.ds(1,1),pl.ds(128*q,128)]=mx.astype(I32)
        for x,r0,nr in ((m2,0,128),(t2,128,16)):
          for hh in range(2):
            y=x[128*hh:128*hh+128].T[:nr]
            rows=pl.ds(144*hh+r0,nr)
            if c==3:
                a=jnp.floor((y+0.5)*(1/256.0))
                ent[6,rows,:]=a
                ent[7,rows,:]=y-256.0*a
            else:
                h=y.astype(BF).astype(F32)
                ent[2*c,rows,:]=h
                ent[2*c+1,rows,:]=y-h
def unpack_chunks(ent, mm_s, surf, amat0, amat1, bmat0, bmat1, jobs):
    ib=lax.broadcasted_iota(I32,(256,128),0).astype(F32).astype(BF)
    ia=lax.broadcasted_iota(I32,(W,128),0).astype(F32).astype(BF)
    one=jnp.ones((256,128),BF); zb=jnp.zeros((256,128),BF); za=jnp.zeros((W,128),BF)
    def row(k,j,h): return jnp.broadcast_to(ent[k,pl.ds(144*h+j,1),:],(16,128))
    def chunk(i,n):
        lo=mm_s[0,i*SL]; hi=mm_s[1,i*SL]
        for q in range(1,SL):
            lo=jnp.minimum(lo,mm_s[0,i*SL+q]); hi=jnp.maximum(hi,mm_s[1,i*SL+q])
        base=(lo//8)*8
        def add(w,n):
            jobs[0,n]=i
            jobs[1,n]=base+w*W
            return n+1
        return lax.fori_loop(0,jnp.where(hi>=0,(hi-base)//W+1,0),add,n)
    n=lax.fori_loop(0,144//SL,chunk,0)
    for k in range(3):
        jobs[0,n+k]=0
        jobs[1,n+k]=AR-W
    def make(k,amat,bmat):
        i=jobs[0,k]; a0=jobs[1,k].astype(F32)
        for j in range(SL):
            for h in range(2):
                cols=pl.ds((2*j+h)*128,128)
                bb=row(7,i*SL+j,h).astype(BF)
                bmat[:,cols]=jnp.where(ib==jnp.tile(bb,(16,1)),one,zb)
                ab=(row(6,i*SL+j,h)-a0).astype(BF)
                m=ia==jnp.tile(ab,(W//16,1))
                for q in range(6):
                    v=row(q,i*SL+j,h).astype(BF)
                    amat[pl.ds(q*W,W),cols]=jnp.where(m,jnp.tile(v,(W//16,1)),za)
    def add_product(k,amat,bmat):
        a0=pl.multiple_of(jobs[1,k],8)
        r=lax.dot_general(amat[...],bmat[...],(((1,),(1,)),((),())),preferred_element_type=F32)
        for c in range(3):
            surf[c,pl.ds(a0,W),:]+=r[2*c*W:(2*c+1)*W]+r[(2*c+1)*W:(2*c+2)*W]
    make(0,amat0,bmat0)
    def pair(t,carry):
        make(2*t+1,amat1,bmat1)
        add_product(2*t,amat0,bmat0)
        make(2*t+2,amat0,bmat0)
        add_product(2*t+1,amat1,bmat1)
        return carry
    lax.fori_loop(0,(n+1)//2,pair,0)
NXD,NYD=135,405

def edges(vel, mask_ref, xe_ref, ye_ref):
    for s,x in ((0,0),(1,NXD-1)):
        M=mask_ref[0:8,:] if s==0 else mask_ref[NXD-8:NXD,:]
        j=0 if s==0 else 7
        m=jnp.broadcast_to(M[j:j+1,:],(8,NYD)).astype(F32)
        for c in range(2): xe_ref[s,c]=vel[c,x]*m
    ye_ref[...]=jnp.zeros_like(ye_ref)
    lane=lax.broadcasted_iota(I32,(8,128),1)
    def block(x0,first,M):
        ma=M[:,0:1]; mb=M[:,NYD-1:NYD]
        static=isinstance(x0,int)
        q=x0//128 if static else 0
        o=x0%128
        for c in range(2):
            lo=jnp.zeros((8,128),F32); hi=lo; fold=lo
            for j in range(first,8):
                v=vel[c,x0+j]
                a=v[:,0:1]*ma[j:j+1,:]
                b=v[:,NYD-1:NYD]*mb[j:j+1,:]
                lo=jnp.where(lane==j,a,lo); hi=jnp.where(lane==j,b,hi); fold=jnp.where(lane==7-j,-b,fold)
            f=pltpu.roll(fold,(127-x0)%128 if static else (127-x0),1)
            lo=pltpu.roll(lo,o,1); hi=pltpu.roll(hi,o,1)
            if static and x0==127:
                ye_ref[0,c,1]=jnp.where(lane<7,lo,0.0); ye_ref[1,c,1]=jnp.where(lane<7,hi,0.0)
                ye_ref[2,c,0]+=f
            elif static and x0==0:
                ye_ref[0,c,0]+=lo; ye_ref[1,c,0]+=hi
                ye_ref[2,c,1]+=jnp.where(lane<7,f,0.0); ye_ref[2,c,0]+=jnp.where(lane==127,f,0.0)
            else:
                ye_ref[0,c,0]+=lo; ye_ref[1,c,0]+=hi; ye_ref[2,c,0]+=f
    def rows(x0): return mask_ref[pl.ds(x0,8),:].astype(F32)
    block(0,0,rows(0))
    def body(i,carry):
        x0=pl.multiple_of(8*i,8)
        block(x0,0,rows(x0))
        return carry
    lax.fori_loop(1,16,body,0)
    block(127,1,mask_ref[NXD-8:NXD,:].astype(F32))

def stencil(vel, thick, cor, mask, xlo, xhi, ylo, yhi, south_scale, put, put_fac):
    sub=lax.broadcasted_iota(I32,(8,NYD),0)
    def mrow(M,j): return jnp.broadcast_to(M[j:j+1,:],(8,NYD))
    def rows8(ref,x0): return ref[pl.ds(x0,8),:].astype(F32)
    M_end=mask[NXD-8:NXD,:].astype(F32)[1:8]; C_end=cor[NXD-8:NXD,:][1:8]
    def block(x0,n,prev,cur,last):
        M=M_end if last else rows8(mask,x0); C=C_end if last else rows8(cor,x0)
        if not last:
            Mn=M_end if isinstance(x0,int) else rows8(mask,pl.multiple_of(x0+8,8))
        q=x0//128 if isinstance(x0,int) else 0
        o=(128-x0%128)%128
        lo=[jnp.where(south_scale>0,pltpu.roll(ylo[c,q],o,1),0.0) for c in range(2)]
        hi=[pltpu.roll(yhi[c,q],o,1) for c in range(2)]
        for j in range(n):
            x=x0+j
            th=thick[x]; inv=1.0/th
            g=0.6/(th+pltpu.roll(th,7,0))
            m1=mrow(M,j); cj=mrow(C,j)
            put_fac(x,M[j:j+1,:]*inv[0:1,:])
            if last and j==n-1: nx=[xhi[c] for c in range(2)]
            else:
                mn=mrow(M,j+1) if j+1<n else mrow(Mn,0)
                nx=[vel[c,x+1]*mn for c in range(2)]
            for c in range(2):
                m=cur[c]
                north=jnp.concatenate([m[:,1:],hi[c][:,j:j+1]],axis=1)
                south=jnp.concatenate([lo[c][:,j:j+1],m[:,:-1]],axis=1)
                lap=(nx[c]+prev[c])+(north+south)-4.0*m
                D=jnp.where(sub==7,0.1*m,g*(m-pltpu.roll(m,7,0)))
                ab=jnp.where(sub==0,0.0,pltpu.roll(D,1,0))
                turn=cj*cur[1] if c==0 else -cj*cur[0]
                put(c,x,(m+turn+0.2*lap+(ab-D)*inv)*m1)
            prev,cur=cur,nx
        return prev,cur
    m0=jnp.broadcast_to(rows8(mask,0)[0:1,:],(8,NYD))
    prev=[xlo[c] for c in range(2)]; cur=[vel[c,0]*m0 for c in range(2)]
    def body(i,st):
        p,c=block(pl.multiple_of(8*i,8),8,list(st[0]),list(st[1]),False)
        return tuple(p),tuple(c)
    st=lax.fori_loop(0,15,body,(tuple(prev),tuple(cur)))
    st=block(120,8,list(st[0]),list(st[1]),False)
    block(128,7,list(st[0]),list(st[1]),True)

def stencil_kernel(pos_ref,vel,thick,cor,mask,xh,yh,out,fac):
    ss=jnp.where(pos_ref[2]==0,0.0,1.0).astype(F32)
    def put(c,x,v): out[c,x]=v
    def put_fac(x,v): fac[x]=jnp.broadcast_to(v,(2,NYD))
    stencil(vel,thick,cor,mask,xh.at[0],xh.at[1],yh.at[0],yh.at[1],ss,put,put_fac)
V=pl.BlockSpec(memory_space=pltpu.VMEM); SM=pl.BlockSpec(memory_space=pltpu.SMEM)


V = pl.BlockSpec(memory_space=pltpu.VMEM)
ANY = pl.BlockSpec(memory_space=pl.ANY)
SM = pl.BlockSpec(memory_space=pltpu.SMEM)


def pack_edge_kernel(pos, stress_hbm, tile_hbm, cell_hbm, weight_hbm, vel_hbm, mask_hbm,
                     main_hbm, tail_hbm, xe_hbm, ye_hbm,
                     stress, tile, cell, weight, vel, mask, main, tail, xe, ye, key_s, val_s, tr_s, isem, osem):
    pairs = ((tile_hbm, tile), (cell_hbm, cell), (weight_hbm, weight), (stress_hbm, stress), (vel_hbm, vel), (mask_hbm, mask))
    loads = [pltpu.make_async_copy(a, b, isem.at[k]) for k, (a, b) in enumerate(pairs)]
    for copy in loads:
        copy.start()
    for copy in loads[:4]:
        copy.wait()
    pack_kernel(pos, stress, tile, cell, weight, main, tail, key_s, val_s, tr_s)
    outs = ((main, main_hbm), (tail, tail_hbm), (xe, xe_hbm), (ye, ye_hbm))
    stores = [pltpu.make_async_copy(a, b, osem.at[k]) for k, (a, b) in enumerate(outs)]
    for copy in stores[:2]:
        copy.start()
    for copy in loads[4:]:
        copy.wait()
    edges(vel, mask, xe, ye)
    for copy in stores[2:]:
        copy.start()
    for copy in stores:
        copy.wait()


def pack_edge(pos, stress, tile, cell, weight, vel, mask):
    D = pltpu.SemaphoreType.DMA
    S = jax.ShapeDtypeStruct
    args = (stress.reshape(2, 72, 128).transpose(1, 0, 2), tile.reshape(72, 128), cell.reshape(72, 128),
            weight.reshape(72, 128), vel, mask)
    outs = (S((256, 4, 128), F32), S((256, 1, 128), F32), S((2, 2, 8, NYD), F32), S((3, 2, 2, 8, 128), F32))
    return pl.pallas_call(
        pack_edge_kernel,
        out_shape=outs,
        in_specs=[SM] + [ANY] * 6,
        out_specs=(ANY,) * 4,
        scratch_shapes=[pltpu.VMEM(a.shape, a.dtype) for a in args + outs] + [
            pltpu.VMEM((72, 128), I32), pltpu.VMEM((3, 72, 128), F32), pltpu.VMEM((128, 128), F32), D((6,)), D((4,))],
        compiler_params=pltpu.CompilerParams(vmem_limit_bytes=60 << 20),
    )(pos, *args)


def coords(d):
    return d // 128, d // 8 % 16, d % 8


def exchange_kernel(main, tail, xe, ye, rec, rtail, xh, yh, lsem, ssem, rsem, xs, xr, ys, yr):
    comp, ox, oy = lax.axis_index("comp"), lax.axis_index("ox"), lax.axis_index("oy")
    me = comp * 128 + ox * 8 + oy
    p = comp * 16 + ox
    barrier = pltpu.get_barrier_semaphore()

    def greet(i, carry):
        pl.semaphore_signal(barrier, inc=1, device_id=coords((me + i) % 256), device_id_type=MESH)
        return carry

    lax.fori_loop(1, 256, greet, 0)
    own = [
        pltpu.make_async_copy(main.at[me], rec.at[me], lsem.at[0]),
        pltpu.make_async_copy(tail.at[me], rtail.at[me], lsem.at[1]),
    ]
    for copy in own:
        copy.start()
    pl.semaphore_wait(barrier, 255)

    def remote(src, dst, ss, rs, pp, oyy):
        return pltpu.make_async_remote_copy(
            src_ref=src, dst_ref=dst, send_sem=ss, recv_sem=rs,
            device_id=(pp // 16, pp % 16, oyy), device_id_type=MESH)

    west, east = (p + 31) % 32, (p + 1) % 32
    x_low = remote(xe.at[0], xh.at[1], xs.at[0], xr.at[1], west, oy)
    x_high = remote(xe.at[1], xh.at[0], xs.at[1], xr.at[0], east, oy)
    y_low = remote(ye.at[0], yh.at[1], ys.at[0], yr.at[1], p, (oy + 7) % 8)
    y_high = remote(ye.at[1], yh.at[0], ys.at[1], yr.at[0], p, (oy + 1) % 8)
    fold = remote(ye.at[2], yh.at[1], ys.at[2], yr.at[1], 31 - p, oy)
    x_low.start()
    x_high.start()

    @pl.when(oy > 0)
    def _():
        y_low.start()

    @pl.when(oy < 7)
    def _():
        y_high.start()

    @pl.when(oy == 7)
    def _():
        fold.start()

    def send(i, carry):
        d = (me + i) % 256
        dev = coords(d)
        pltpu.make_async_remote_copy(
            src_ref=main.at[d], dst_ref=rec.at[me], send_sem=ssem.at[0], recv_sem=rsem.at[0],
            device_id=dev, device_id_type=MESH).start()
        pltpu.make_async_remote_copy(
            src_ref=tail.at[d], dst_ref=rtail.at[me], send_sem=ssem.at[1], recv_sem=rsem.at[1],
            device_id=dev, device_id_type=MESH).start()
        return carry

    lax.fori_loop(1, 256, send, 0)
    for copy in own:
        copy.wait()
    x_low.wait()
    x_high.wait()

    @pl.when(oy > 0)
    def _():
        y_low.wait_send()
        pltpu.make_async_copy(ye.at[1], yh.at[0], yr.at[0]).wait()

    @pl.when(oy < 7)
    def _():
        y_high.wait_send()

    @pl.when(oy == 7)
    def _():
        fold.wait_send()

    pltpu.make_async_copy(ye.at[0], yh.at[1], yr.at[1]).wait()
    n = pl.ds(0, 255)
    pltpu.make_async_copy(main.at[n], rec.at[n], ssem.at[0]).wait()
    pltpu.make_async_copy(tail.at[n], rtail.at[n], ssem.at[1]).wait()
    pltpu.make_async_copy(main.at[n], rec.at[n], rsem.at[0]).wait()
    pltpu.make_async_copy(tail.at[n], rtail.at[n], rsem.at[1]).wait()


def exchange(main, tail, xe, ye):
    shapes = [jax.ShapeDtypeStruct(a.shape, a.dtype) for a in (main, tail, xe)]
    shapes.append(jax.ShapeDtypeStruct((2, 2, 2, 8, 128), F32))
    D = pltpu.SemaphoreType.DMA
    return pl.pallas_call(
        exchange_kernel,
        out_shape=tuple(shapes),
        in_specs=[ANY] * 4,
        out_specs=(ANY,) * 4,
        scratch_shapes=[D((2,)), D((2,)), D((2,)), D((2,)), D((2,)), D((3,)), D((2,))],
        compiler_params=pltpu.CompilerParams(collective_id=0, has_side_effects=True),
    )(main, tail, xe, ye)


ROWS = 15


def finish_kernel(pos, rec_hbm, rtail_hbm, axes_hbm, vel_hbm, thick_hbm, cor_hbm, mask_hbm, xh_hbm, yh_hbm, out_hbm,
                  vel, thick, cor, mask, xh, yh, rec, rtail, ent, mm_v, mm_s, amat0, amat1, bmat0, bmat1, jobs, surf, flat, step, axes, fac, sem, isem, osem, lsem):
    first = [
        pltpu.make_async_copy(rec_hbm, rec, isem.at[3]),
        pltpu.make_async_copy(rtail_hbm, rtail, isem.at[4]),
    ]
    for copy in first:
        copy.start()
    pairs = ((axes_hbm, axes), (vel_hbm, vel), (thick_hbm, thick), (cor_hbm, cor), (mask_hbm, mask), (xh_hbm, xh), (yh_hbm, yh))
    loads = [pltpu.make_async_copy(a, b, lsem.at[k]) for k, (a, b) in enumerate(pairs)]
    for copy in loads:
        copy.start()
    for copy in first:
        copy.wait()
    unpack_prepare(rec, rtail, ent, mm_v)
    copy = pltpu.make_async_copy(mm_v, mm_s, sem)
    copy.start()
    surf[...] = jnp.zeros_like(surf)
    copy.wait()
    unpack_chunks(ent, mm_s, surf, amat0, amat1, bmat0, bmat1, jobs)
    for c in range(3):
        for h in range(2):
            flat[pl.ds(h, 216, stride=2), c, :] = surf[c, 0:216, 128 * h:128 * h + 128]
    for copy in loads:
        copy.wait()
    stencil_kernel(pos, vel, thick, cor, mask, xh, yh, step, fac)

    def row(x):
        r, o = 405 * x // 128, 405 * x % 128
        lane = lax.broadcasted_iota(I32, (4, 128), 1)
        t = [pltpu.roll(flat[r + k], (128 - o) % 128, 1) for k in range(5)]
        cut = lane < 128 - o
        for q in range(4):
            w = min(128, NYD - 128 * q)
            s = jnp.where(cut, t[q], t[q + 1])
            cols = pl.ds(128 * q, w)
            total = jnp.zeros((2, w), F32)
            for c in range(3):
                total += axes[c, x, :, cols] * jnp.broadcast_to(s[c:c + 1, :w], (2, w))
            total = total * fac[x, :, cols]
            for i in range(2):
                step[i, x, 0:1, cols] += total[i:i + 1, :]

    def out_copy(g):
        rows = pl.ds(g * ROWS, ROWS)
        return pltpu.make_async_copy(step.at[:, rows], out_hbm.at[:, rows], osem.at[g])

    def group(g, carry):
        def one(k, carry):
            row(g * ROWS + k)
            return carry

        lax.fori_loop(0, ROWS, one, 0, unroll=3)
        out_copy(g).start()
        return carry

    lax.fori_loop(0, NXD // ROWS, group, 0)

    def drain(g, carry):
        out_copy(g).wait()
        return carry

    lax.fori_loop(0, NXD // ROWS, drain, 0)


def finish(pos, rec, rtail, axes, vel, thick, cor, mask, xh, yh):
    D = pltpu.SemaphoreType.DMA
    return pl.pallas_call(
        finish_kernel,
        out_shape=jax.ShapeDtypeStruct((2, NXD, 8, NYD), F32),
        in_specs=[SM] + [ANY] * 9,
        out_specs=ANY,
        scratch_shapes=[pltpu.VMEM(a.shape, a.dtype) for a in (vel, thick, cor, mask, xh, yh)] + [
            pltpu.VMEM((256, 4, 128), F32), pltpu.VMEM((256, 1, 128), F32),
            pltpu.VMEM((8, 288, 128), F32), pltpu.VMEM((8, 256), I32), pltpu.SMEM((8, 256), I32),
            pltpu.VMEM((6 * W, SL * 256), BF), pltpu.VMEM((6 * W, SL * 256), BF),
            pltpu.VMEM((256, SL * 256), BF), pltpu.VMEM((256, SL * 256), BF), pltpu.SMEM((2, 64), I32),
            pltpu.VMEM((3, AR, 256), F32), pltpu.VMEM((432, 4, 128), F32),
            pltpu.VMEM((2, NXD, 8, NYD), F32), pltpu.VMEM((3, NXD, 2, NYD), F32), pltpu.VMEM((NXD, 2, NYD), F32),
            D, D((5,)), D((NXD // ROWS,)), D((7,)),
        ],
        compiler_params=pltpu.CompilerParams(vmem_limit_bytes=60 << 20),
    )(pos, rec, rtail, axes, vel, thick, cor, mask, xh, yh)


def shards(atmos_stress, route_tile, route_cell, route_weight, velocity, thickness, coriolis, ocean_axes, ocean_mask):
    vel = velocity.transpose(0, 2, 1, 3)
    pos = jnp.stack([lax.axis_index("comp"), lax.axis_index("ox"), lax.axis_index("oy")]).astype(I32)
    main, tail, xe, ye = pack_edge(pos, atmos_stress, route_tile, route_cell, route_weight, vel, ocean_mask)
    rec, rtail, xh, yh = exchange(main, tail, xe, ye)
    out = finish(pos, rec, rtail, ocean_axes.transpose(1, 2, 0, 3), vel, thickness.transpose(1, 0, 2), coriolis,
                 ocean_mask, xh, yh)
    return out.transpose(0, 2, 1, 3)


def solution(mesh):
    return jax.shard_map(
        shards,
        mesh=mesh,
        in_specs=(
            P(None, ("comp", "ox", "oy")),
            P(("comp", "ox", "oy"), None),
            P(("comp", "ox", "oy")),
            P(("comp", "ox", "oy")),
            P(None, None, ("comp", "ox"), "oy"),
            P(None, ("comp", "ox"), "oy"),
            P(("comp", "ox"), "oy"),
            P(None, None, ("comp", "ox"), "oy"),
            P(("comp", "ox"), "oy"),
        ),
        out_specs=P(None, None, ("comp", "ox"), "oy"),
        check_vma=False,
    )
```

profile of v0, /device:TPU:1, one launch (start us, length us, event | category | flops | bytes accessed | tf_op | source)
XLA Modules:
  0.0 83.8 jit_solution(15090265866610377814)
XLA Ops:
  0.0 0.7 pad_add_fusion.pos
  0.7 12.9 %shard_map.91 = (f32[256,4,128]{2,1,0:T(4,128)}, f32[256,1,128]{2,1,0:T(1,128)}, f32[2,2,8,405]{3,2,1,0:T(8,128)}, f32[3,2,2,8,128]{4,3,2,1,0:T(8,128)}) custom-call(s32[3]{0:T(128)} %pad_add_fusion.pos, f32[72,2,128]{2,1,0:T(2,128)} %bitcast.17, s32[72,128]{1,0:T(8,128)} %bitcast.18, s32[72,128]{1,0:T(8,128)} %bitcast.19, f32[72,128]{1,0:T(8,128)} %bitcast.20, ...), custom_call_target="tpu_custom_call" | custom-call | tf_op jit(solution)/shard_map/pallas_call | solution.py:342
  13.6 36.9 %shard_map.92 = (f32[256,4,128]{2,1,0:T(4,128)}, f32[256,1,128]{2,1,0:T(1,128)}, f32[2,2,8,405]{3,2,1,0:T(8,128)}, f32[2,2,2,8,128]{4,3,2,1,0:T(8,128)}) custom-call(f32[256,4,128]{2,1,0:T(4,128)} %get-tuple-element.13.main, f32[256,1,128]{2,1,0:T(1,128)} %get-tuple-element.14.tail, f32[2,2,8,405]{3,2,1,0:T(8,128)} %get-tuple-element.15.xe, ...), custom_call_target="tpu_custom_call" | custom-call | tf_op jit(solution)/shard_map/pallas_call | solution.py:444
  50.5 33.3 %shard_map.93 = f32[2,135,8,405]{3,2,1,0:T(8,128)} custom-call(s32[3]{0:T(128)} %pad_add_fusion.pos, f32[256,4,128]{2,1,0:T(4,128)} %get-tuple-element.17.rec_hbm, f32[256,1,128]{2,1,0:T(1,128)} %get-tuple-element.18.rtail_hbm, f32[3,135,2,405]{3,2,1,0:T(2,128)} %bitcast.16, f32[2,135,8,405]{3,2,1,0:T(8,128)} %bitcast.14, f32[135,8,405]{2,1,0:T(8,128)} %bitcast.15, ...), custom_call_target="tpu_custom_call" | custom-call | tf_op jit(solution)/shard_map/pallas_call | solution.py:524
where the time goes:
time: 84 us; the launch traced here: 83.8 us
  Pallas kernels  83.1 us (99%)
    pallas_call x1, Pallas kernels, exchange(): pl.pallas_call(exchange_kernel, out_shape=tuple(shapes), in_specs=[ANY] *...  36.9 us
    pallas_call x1, Pallas kernels, finish(): pl.pallas_call(finish_kernel, out_shape=jax.ShapeDtypeStruct((2, NXD, 8,...  33.3 us
    pallas_call x1, Pallas kernels, pack_edge(): pl.pallas_call(pack_edge_kernel, out_shape=outs, in_specs=[SM] + [ANY] *...  12.9 us

commit v1 on v0

--- a/solution.py
+++ b/solution.py
@@ -11,6 +11,7 @@
 F32 = jnp.float32
 I32 = jnp.int32
 MESH = pl.DeviceIdType.MESH
+LOGICAL = pl.DeviceIdType.LOGICAL
 FN=[[1,0,0],[0,1,0],[-1,0,0],[0,-1,0],[0,0,1],[0,0,-1]]
 FA=[[0,1,0],[-1,0,0],[0,-1,0],[1,0,0],[0,1,0],[0,1,0]]
 FB=[[0,0,1],[0,0,1],[0,0,1],[0,0,1],[-1,0,0],[1,0,0]]
@@ -350,10 +351,6 @@
     )(pos, *args)
 
 
-def coords(d):
-    return d // 128, d // 8 % 16, d % 8
-
-
 def exchange_kernel(main, tail, xe, ye, rec, rtail, xh, yh, lsem, ssem, rsem, xs, xr, ys, yr):
     comp, ox, oy = lax.axis_index("comp"), lax.axis_index("ox"), lax.axis_index("oy")
     me = comp * 128 + ox * 8 + oy
@@ -361,10 +358,11 @@
     barrier = pltpu.get_barrier_semaphore()
 
     def greet(i, carry):
-        pl.semaphore_signal(barrier, inc=1, device_id=coords((me + i) % 256), device_id_type=MESH)
+        for k in range(1, 6):
+            pl.semaphore_signal(barrier, inc=1, device_id=(me + 5 * i + k) % 256, device_id_type=LOGICAL)
         return carry
 
-    lax.fori_loop(1, 256, greet, 0)
+    lax.fori_loop(0, 51, greet, 0)
     own = [
         pltpu.make_async_copy(main.at[me], rec.at[me], lsem.at[0]),
         pltpu.make_async_copy(tail.at[me], rtail.at[me], lsem.at[1]),
@@ -400,17 +398,17 @@
         fold.start()
 
     def send(i, carry):
-        d = (me + i) % 256
-        dev = coords(d)
-        pltpu.make_async_remote_copy(
-            src_ref=main.at[d], dst_ref=rec.at[me], send_sem=ssem.at[0], recv_sem=rsem.at[0],
-            device_id=dev, device_id_type=MESH).start()
-        pltpu.make_async_remote_copy(
-            src_ref=tail.at[d], dst_ref=rtail.at[me], send_sem=ssem.at[1], recv_sem=rsem.at[1],
-            device_id=dev, device_id_type=MESH).start()
+        for k in range(1, 6):
+            d = (me + 5 * i + k) % 256
+            pltpu.make_async_remote_copy(
+                src_ref=main.at[d], dst_ref=rec.at[me], send_sem=ssem.at[0], recv_sem=rsem.at[0],
+                device_id=d, device_id_type=LOGICAL).start()
+            pltpu.make_async_remote_copy(
+                src_ref=tail.at[d], dst_ref=rtail.at[me], send_sem=ssem.at[1], recv_sem=rsem.at[1],
+                device_id=d, device_id_type=LOGICAL).start()
         return carry
 
-    lax.fori_loop(1, 256, send, 0)
+    lax.fori_loop(0, 51, send, 0)
     for copy in own:
         copy.wait()
     x_low.wait()

time: 84 us -> 81.1 us (0.965)
  the two profiles are of different devices: /device:TPU:1 before, /device:TPU:30 now
where the time goes in v1:
time: 81.1 us; the launch traced here: 79.6 us
  Pallas kernels  78.9 us (97%)
    pallas_call x1, Pallas kernels, finish(): pl.pallas_call(finish_kernel, out_shape=jax.ShapeDtypeStruct((2, NXD, 8,...  34.8 us
    pallas_call x1, Pallas kernels, exchange(): pl.pallas_call(exchange_kernel, out_shape=tuple(shapes), in_specs=[ANY] *...  31.2 us
    pallas_call x1, Pallas kernels, pack_edge(): pl.pallas_call(pack_edge_kernel, out_shape=outs, in_specs=[SM] + [ANY] *...  12.9 us

profile of v1, /device:TPU:30, one launch (start us, length us, event | category | flops | bytes accessed | tf_op | source)
XLA Modules:
  0.0 79.6 jit_solution(2955559951897876343)
XLA Ops:
  0.0 0.7 pad_add_fusion.pos
  0.7 12.9 %shard_map.91 = (f32[256,4,128]{2,1,0:T(4,128)}, f32[256,1,128]{2,1,0:T(1,128)}, f32[2,2,8,405]{3,2,1,0:T(8,128)}, f32[3,2,2,8,128]{4,3,2,1,0:T(8,128)}) custom-call(s32[3]{0:T(128)} %pad_add_fusion.pos, f32[72,2,128]{2,1,0:T(2,128)} %bitcast.17, s32[72,128]{1,0:T(8,128)} %bitcast.18, s32[72,128]{1,0:T(8,128)} %bitcast.19, f32[72,128]{1,0:T(8,128)} %bitcast.20, ...), custom_call_target="tpu_custom_call" | custom-call | tf_op jit(solution)/shard_map/pallas_call | solution.py:343
  13.6 31.2 %shard_map.92 = (f32[256,4,128]{2,1,0:T(4,128)}, f32[256,1,128]{2,1,0:T(1,128)}, f32[2,2,8,405]{3,2,1,0:T(8,128)}, f32[2,2,2,8,128]{4,3,2,1,0:T(8,128)}) custom-call(f32[256,4,128]{2,1,0:T(4,128)} %get-tuple-element.13.main, f32[256,1,128]{2,1,0:T(1,128)} %get-tuple-element.14.tail, f32[2,2,8,405]{3,2,1,0:T(8,128)} %get-tuple-element.15.xe, ...), custom_call_target="tpu_custom_call" | custom-call | tf_op jit(solution)/shard_map/pallas_call | solution.py:442
  44.8 34.8 %shard_map.93 = f32[2,135,8,405]{3,2,1,0:T(8,128)} custom-call(s32[3]{0:T(128)} %pad_add_fusion.pos, f32[256,4,128]{2,1,0:T(4,128)} %get-tuple-element.17.rec_hbm, f32[256,1,128]{2,1,0:T(1,128)} %get-tuple-element.18.rtail_hbm, f32[3,135,2,405]{3,2,1,0:T(2,128)} %bitcast.16, f32[2,135,8,405]{3,2,1,0:T(8,128)} %bitcast.14, f32[135,8,405]{2,1,0:T(8,128)} %bitcast.15, ...), custom_call_target="tpu_custom_call" | custom-call | tf_op jit(solution)/shard_map/pallas_call | solution.py:522
